TPU v7x, 32 devices: a whole 2x2x4 slice. The times are simulated.
32 devices in a mesh: kvh: 2 (over x), ctx: 16 (over z, y, core).
Axes of the slice: x: 2, y: 2, z: 4, core: 2. Of those that a mesh axis runs over, the one named last changes fastest.
Arguments:
- queries: bfloat16 [512, 32, 128], P('ctx', 'kvh'), parts along dimension 1, may hold values from -6 to 6
- cache_keys: bfloat16 [16384, 256], P('ctx', 'kvh'), parts along dimension 1, may hold values from -6 to 6
- cache_values: bfloat16 [16384, 256], P('ctx', 'kvh'), parts along dimension 1, may hold values from -6 to 6
- span_offset: int32 [1], replicated, may hold values from 0 to 8191
- positions: int32 [512], replicated, may hold values from 0 to 8191
Outputs:
- attended: bfloat16 [512, 32, 128], P('ctx', 'kvh'), parts along dimension 1
There are 2 independent parts, one for each index of `kvh`. A program takes and returns all parts, laid end to end along the dimension named above; an argument that names none is the same for every part. Nothing has to cross between parts.
All inputs are finite; a program needn't handle non-finite values.
Results may differ from a plain program's by a relative error of at most 0.0029.
Values may be sent and summed in bfloat16 or wider, within the bound.
No kernel may reach another device: no remote copies, remote signals or barrier semaphores. Data moves between devices by JAX's collectives and lax.ppermute only.
A program may use at most 64 MiB of HBM per device.

v0:
```python
import functools

import jax
import jax.numpy as jnp
from jax import lax
from jax.experimental import pallas as pl
from jax.experimental.pallas import tpu as pltpu
from jax.sharding import PartitionSpec as P


masked_floor = -1e30
log2_e = 1.4426950408889634
inner = 4
extra_rows = 16
code_span = 240.0
code_low = -120.0


def block_update(state, query, keys, values, limit, scale):
    shard_keys, width = keys.shape
    scores = lax.dot_general(keys, query, (((1,), (1,)), ((), ())), preferred_element_type=jnp.float32)
    key_position = lax.broadcasted_iota(jnp.int32, scores.shape, 0)
    scores = jnp.where(key_position <= limit, scores, masked_floor)
    shard_max = jnp.max(scores, axis=0, keepdims=True)
    weights = jnp.exp2((scores - shard_max) * scale).astype(jnp.bfloat16)
    ones = jnp.ones((extra_rows, shard_keys), jnp.bfloat16)
    values_t = jnp.concatenate([values.T, ones], axis=0)
    sums = lax.dot_general(values_t, weights, (((1,), (0,)), ((), ())), preferred_element_type=jnp.float32)
    num, den = sums[:width], sums[width : width + 1]
    if state is None:
        return shard_max, den, num
    top, run_den, run_num = state
    new_top = jnp.maximum(top, shard_max)
    keep = jnp.exp2((top - new_top) * scale)
    fresh = jnp.exp2((shard_max - new_top) * scale)
    return new_top, run_den * keep + den * fresh, run_num * keep + num * fresh


def encode(values, level):
    _, lanes = values.shape
    size = jnp.abs(values)
    peak = jnp.maximum(jnp.max(size, axis=0, keepdims=True), 1e-30).astype(jnp.bfloat16).astype(jnp.float32)
    code = jnp.exp2(size * (code_span / peak) + code_low)
    code = jnp.where(values < 0, -code, code)
    high = level.astype(jnp.bfloat16).astype(jnp.float32)
    rest = level - high
    middle = rest.astype(jnp.bfloat16).astype(jnp.float32)
    row = lax.broadcasted_iota(jnp.int32, (extra_rows, lanes), 0)
    tail = jnp.where(row == 0, high, jnp.where(row == 1, middle, jnp.where(row == 2, rest - middle, peak)))
    return code.astype(jnp.bfloat16), tail.astype(jnp.bfloat16)


def decode(codes, tail):
    codes, tail = codes.astype(jnp.float32), tail.astype(jnp.float32)
    level = tail[0:1] + tail[1:2] + tail[2:3]
    size = (jnp.log2(jnp.abs(codes)) - code_low) * (tail[3:4] * (1.0 / code_span))
    return jnp.where(codes < 0, -size, size), level


def attend_kernel(scale, rows_of, has_state, form, own_rows, *refs):
    limits_ref, q_ref = refs[:2]
    pair_refs = refs[2 : 2 + len(rows_of)]
    rest = refs[2 + len(rows_of) :]
    query = q_ref[...]
    state = None
    if has_state:
        state = tuple(ref[...] for ref in rest[:3])
        rest = rest[3:]
    for row, pair_ref in zip(rows_of, pair_refs):
        shard_keys = pair_ref.shape[0] // 2
        state = block_update(
            state, query, pair_ref[:shard_keys, :], pair_ref[shard_keys:, :], limits_ref[row : row + 1, :], scale
        )
    if form == "state":
        for ref, value in zip(rest, state):
            ref[...] = value
        return
    top, den, num = state
    width = num.shape[0]
    level = top * scale + jnp.log2(den)
    out = num * (1.0 / den)
    rest = list(rest)
    if own_rows:
        out_ref, level_ref = rest[:2]
        rest = rest[2:]
        out_ref[...] = out[:, :own_rows]
        level_ref[...] = level[:, :own_rows]
    if rest:
        code, tail = encode(out, level)
        rest[0][:width, :] = code
        rest[0][width:, :] = tail


def merge_kernel(count, *refs):
    own_ref, own_level_ref = refs[:2]
    parts, out_ref = refs[2 : 1 + count], refs[1 + count]
    width = own_ref.shape[0]
    values, levels = [own_ref[...]], [own_level_ref[...]]
    for part in parts:
        value, level = decode(part[:width, :], part[width:, :])
        values.append(value)
        levels.append(level)
    top = functools.reduce(jnp.maximum, levels)
    factors = [jnp.exp2(level - top) for level in levels]
    inverse = 1.0 / functools.reduce(jnp.add, factors)
    num = functools.reduce(jnp.add, [value * (factor * inverse) for value, factor in zip(values, factors)])
    out_ref[...] = num.T.astype(out_ref.dtype)


def local(size, queries, cache_keys, cache_values, span_offset, positions):
    own_tokens, head_count, head_width = queries.shape
    shard_keys = cache_keys.shape[0]
    outer = size // inner
    rows = own_tokens * head_count
    me = lax.axis_index("ctx")
    place, owner = me % inner, me // inner
    scale = head_width ** (-0.5) * log2_e

    def swap(array, step):
        return lax.ppermute(array, "ctx", [(i, i ^ step) for i in range(size)])

    query = queries.reshape(rows, head_width)
    own_pair = jnp.concatenate([cache_keys, cache_values], axis=0)
    far_pair = swap(own_pair, 2)
    got = [query] + [swap(query, inner * k) for k in range(1, outer)]
    near_pair = swap(own_pair, 1)

    per_stage = max(outer // 4, 1)
    stages = [list(range(s, s + per_stage)) for s in range(0, outer, per_stage)]
    stage_rows = rows * per_stage

    limits = (span_offset[0] + positions).reshape(outer, inner, own_tokens)
    limits = lax.dynamic_index_in_dim(limits, place, 1, keepdims=False)
    limits = jnp.concatenate([lax.dynamic_slice_in_dim(limits, owner ^ k, 1, axis=0) for k in range(outer)], axis=0)
    limits = jnp.repeat(limits, head_count, axis=1).reshape(len(stages), 1, stage_rows)
    bases = (me ^ lax.iota(jnp.int32, inner)) * shard_keys
    limits = (limits - bases[None, :, None]).reshape(len(stages) * inner, stage_rows)

    def join(items, axis):
        return items[0] if len(items) == 1 else jnp.concatenate(items, axis=axis)

    vmem = pl.BlockSpec(memory_space=pltpu.VMEM)
    params = pltpu.CompilerParams(vmem_limit_bytes=40 << 20)
    pairs = [own_pair, near_pair]
    stage_query = [join([got[k] for k in stage], 0) for stage in stages]
    stat = jax.ShapeDtypeStruct((1, stage_rows), jnp.float32)
    state_shapes = [stat, stat, jax.ShapeDtypeStruct((head_width, stage_rows), jnp.float32)]
    packed_shape = jax.ShapeDtypeStruct((head_width + extra_rows, stage_rows), jnp.bfloat16)
    own_shapes = [jax.ShapeDtypeStruct((head_width, rows), jnp.float32), jax.ShapeDtypeStruct((1, rows), jnp.float32)]
    chain = [limits]
    states = [None] * len(stages)

    def attend(index, blocks, form):
        own_rows = rows if form == "packed" and index == 0 else 0
        if form == "state":
            shapes = state_shapes
        else:
            shapes = (own_shapes if own_rows else []) + ([packed_shape] if index or per_stage > 1 else [])
        operands = [chain[0], stage_query[index]] + [pairs[b] for b in blocks] + list(states[index] or ())
        results = pl.pallas_call(
            functools.partial(
                attend_kernel, scale, [index * inner + b for b in blocks], states[index] is not None, form, own_rows
            ),
            in_specs=[vmem] * len(operands),
            out_specs=[vmem] * len(shapes),
            out_shape=shapes,
            compiler_params=params,
        )(*operands)
        chain[0], results = lax.optimization_barrier((chain[0], results))
        if form == "state":
            states[index] = results
        return results

    attend(0, [0], "state")
    attend(0, [1], "state")
    for index in range(1, len(stages)):
        attend(index, [0, 1], "state")

    chain[0], far_pair = lax.optimization_barrier((chain[0], far_pair))
    across_pair = swap(far_pair, 1)
    pairs += [far_pair, across_pair]
    parts = [None] * outer

    def send(index, packed):
        for at, k in enumerate(stages[index]):
            if k:
                piece = packed if per_stage == 1 else packed[:, at * rows : (at + 1) * rows]
                parts[k] = swap(piece, inner * k)

    last = len(stages) - 1
    attend(last, [2], "state")
    send(last, attend(last, [3], "packed")[0])
    for index in range(last - 1, 0, -1):
        send(index, attend(index, [2, 3], "packed")[0])
    results = attend(0, [2, 3], "packed")
    if per_stage > 1:
        send(0, results[2])
    merged = pl.pallas_call(
        functools.partial(merge_kernel, outer),
        in_specs=[vmem] * (outer + 1),
        out_specs=vmem,
        out_shape=jax.ShapeDtypeStruct((rows, head_width), jnp.bfloat16),
        compiler_params=params,
        name="merge",
    )(results[0], results[1], *parts[1:])
    return merged.reshape(own_tokens, head_count, head_width)


def solution(mesh):
    in_specs = (P("ctx", "kvh", None), P("ctx", "kvh"), P("ctx", "kvh"), P(), P())
    out_specs = P("ctx", "kvh", None)
    size = mesh.shape["ctx"]

    def body(*args):
        return local(size, *args)

    return jax.shard_map(body, mesh=mesh, in_specs=in_specs, out_specs=out_specs, check_vma=False)
```

profile of v0, /device:TPU:13, one launch (start us, length us, event | category | flops | bytes accessed | tf_op | source)
XLA Modules:
  0.0 44.5 jit_solution(17139437249994447249)
XLA Ops:
  0.0 0.0 copy-start.1
  0.0 0.2 collective-permute-start.1
  0.2 2.3 %collective-permute-start.2 = (bf16[512,128]{1,0:T(8,128)(2,1)}, bf16[512,128]{1,0:T(8,128)(2,1)S(1)}, u32[]{:S(2)}, u32[]{:S(2)}) collective-permute-start(bf16[512,128]{1,0:T(8,128)(2,1)} %bitcast.13), channel_id=1, source_target_pairs={{0,8},{1,9},{2,10},{3,11},{4,12},{5,13},{6,14},{7,15},{8,0},{9,1},... | collective-permute-start | bytes 393224 | tf_op jit(solution)/shard_map/ppermute | solution.py:120
  2.5 0.2 collective-permute-start.3
  2.7 1.0 %constant_dynamic-update-slice_fusion.1 = bf16[2048,128]{1,0:T(8,128)(2,1)S(1)} fusion(bf16[1024,128]{1,0:T(8,128)(2,1)} %param.6), kind=kLoop, calls=%fused_computation.2 | loop fusion | bytes 524288
  3.6 0.0 copy-done.1
  3.7 1.6 %collective-permute-start = (bf16[2048,128]{1,0:T(8,128)(2,1)S(1)}, bf16[2048,128]{1,0:T(8,128)(2,1)S(1)}, u32[]{:S(2)}, u32[]{:S(2)}) collective-permute-start(bf16[2048,128]{1,0:T(8,128)(2,1)S(1)} %constant_dynamic-update-slice_fusion.refs_2_), channel_id=1, source_target_pairs={{0,1},{1,0},{2,3},{3,2},{4,5},{5,4},{6,7},{7,6},{8,9},{9,8},{10,11... | collective-permute-start | bytes 1572872 | tf_op jit(solution)/shard_map/ppermute | solution.py:120
  5.3 0.2 collective-permute-start.4
  5.5 0.0 copy-start.2
  6.2 0.0 copy-done.2
  6.2 0.1 reshape.22
  6.3 0.1 broadcast_in_dim.4
  6.4 0.0 copy-start
  6.4 0.1 sub.27
  6.5 0.1 sub.31
  6.6 0.1 broadcast_subtract_fusion.refs_0_
  6.7 0.6 %copy-done = bf16[32,16,128]{2,1,0:T(8,128)(2,1)S(1)} copy-done((bf16[32,16,128]{2,1,0:T(8,128)(2,1)S(1)}, bf16[32,16,128]{2,1,0:T(8,128)(2,1)}, u32[]{:S(2)}) %copy-start) | copy-done | bytes 131096
  7.3 1.1 %shard_map.55 = (f32[1,512]{1,0:T(1,128)S(1)}, f32[1,512]{1,0:T(1,128)S(1)}, f32[128,512]{1,0:T(8,128)S(1)}) custom-call(s32[16,512]{1,0:T(8,128)S(1)} %broadcast_subtract_fusion.refs_0_, bf16[512,128]{1,0:T(8,128)(2,1)S(1)} %bitcast.15, bf16[2048,128]{1,0:T(8,128)(2,1)S(1)} %constant_dynamic-update-slice_fusion.refs_2_), custom_call_target="tpu_custom_call" | custom-call | tf_op jit(solution)/shard_map/pallas_call | solution.py:160
  8.3 0.0 collective-permute-done.refs_2_.refs_3_
  8.4 1.1 %shard_map.56 = (f32[1,512]{1,0:T(1,128)S(1)}, f32[1,512]{1,0:T(1,128)S(1)}, f32[128,512]{1,0:T(8,128)S(1)}) custom-call(s32[16,512]{1,0:T(8,128)S(1)} %broadcast_subtract_fusion.refs_0_, bf16[512,128]{1,0:T(8,128)(2,1)S(1)} %bitcast.16, bf16[2048,128]{1,0:T(8,128)(2,1)S(1)} %collective-permute-done.refs_2_.refs_3_, f32[1,512]{1,0:T(1,128)S(1)} %get-tuple-element.63.refs_3_, ...), custom_call_target="tpu_custom_call" | custom-call | tf_op jit(solution)/shard_map/pallas_call | solution.py:160
  9.4 0.0 collective-permute-done.1.refs_1_
  9.4 2.0 %shard_map.57 = (f32[1,512]{1,0:T(1,128)S(1)}, f32[1,512]{1,0:T(1,128)S(1)}, f32[128,512]{1,0:T(8,128)S(1)}) custom-call(s32[16,512]{1,0:T(8,128)S(1)} %broadcast_subtract_fusion.refs_0_, bf16[512,128]{1,0:T(8,128)(2,1)S(1)} %collective-permute-done.1.refs_1_, bf16[2048,128]{1,0:T(8,128)(2,1)S(1)} %constant_dynamic-update-slice_fusion.refs_2_, ...), custom_call_target="tpu_custom_call" | custom-call | tf_op jit(solution)/shard_map/pallas_call | solution.py:160
  11.5 0.0 collective-permute-done.2.refs_1_
  11.5 2.0 %shard_map.58 = (f32[1,512]{1,0:T(1,128)S(1)}, f32[1,512]{1,0:T(1,128)S(1)}, f32[128,512]{1,0:T(8,128)S(1)}) custom-call(s32[16,512]{1,0:T(8,128)S(1)} %broadcast_subtract_fusion.refs_0_, bf16[512,128]{1,0:T(8,128)(2,1)S(1)} %collective-permute-done.2.refs_1_, bf16[2048,128]{1,0:T(8,128)(2,1)S(1)} %constant_dynamic-update-slice_fusion.refs_2_, ...), custom_call_target="tpu_custom_call" | custom-call | tf_op jit(solution)/shard_map/pallas_call | solution.py:160
  13.5 0.6 %collective-permute-done.3.refs_1_ = bf16[512,128]{1,0:T(8,128)(2,1)S(1)} collective-permute-done((bf16[512,128]{1,0:T(8,128)(2,1)}, bf16[512,128]{1,0:T(8,128)(2,1)S(1)}, u32[]{:S(2)}, u32[]{:S(2)}) %collective-permute-start.3) | collective-permute-done | bytes 131104 | tf_op jit(solution)/shard_map/ppermute | solution.py:120
  14.0 2.0 %shard_map.59 = (f32[1,512]{1,0:T(1,128)S(1)}, f32[1,512]{1,0:T(1,128)S(1)}, f32[128,512]{1,0:T(8,128)S(1)}) custom-call(s32[16,512]{1,0:T(8,128)S(1)} %broadcast_subtract_fusion.refs_0_, bf16[512,128]{1,0:T(8,128)(2,1)S(1)} %collective-permute-done.3.refs_1_, bf16[2048,128]{1,0:T(8,128)(2,1)S(1)} %constant_dynamic-update-slice_fusion.refs_2_, ...), custom_call_target="tpu_custom_call" | custom-call | tf_op jit(solution)/shard_map/pallas_call | solution.py:160
  16.1 2.6 %collective-permute-done.4.refs_2_ = bf16[2048,128]{1,0:T(8,128)(2,1)S(1)} collective-permute-done((bf16[2048,128]{1,0:T(8,128)(2,1)S(1)}, bf16[2048,128]{1,0:T(8,128)(2,1)S(1)}, u32[]{:S(2)}, u32[]{:S(2)}) %collective-permute-start.4) | collective-permute-done | bytes 524320 | tf_op jit(solution)/shard_map/ppermute | solution.py:120
  18.7 0.9 %collective-permute-start.5 = (bf16[2048,128]{1,0:T(8,128)(2,1)S(1)}, bf16[2048,128]{1,0:T(8,128)(2,1)S(1)}, u32[]{:S(2)}, u32[]{:S(2)}) collective-permute-start(bf16[2048,128]{1,0:T(8,128)(2,1)S(1)} %collective-permute-done.4.refs_2_), channel_id=1, source_target_pairs={{0,1},{1,0},{2,3},{3,2},{4,5},{5,4},{6,7},{7,6},{8,9},{9,8},{10,11... | collective-permute-start | bytes 1572872 | tf_op jit(solution)/shard_map/ppermute | solution.py:120
  19.6 1.1 %shard_map.60 = (f32[1,512]{1,0:T(1,128)S(1)}, f32[1,512]{1,0:T(1,128)S(1)}, f32[128,512]{1,0:T(8,128)S(1)}) custom-call(s32[16,512]{1,0:T(8,128)S(1)} %broadcast_subtract_fusion.refs_0_, bf16[512,128]{1,0:T(8,128)(2,1)S(1)} %collective-permute-done.3.refs_1_, bf16[2048,128]{1,0:T(8,128)(2,1)S(1)} %collective-permute-done.4.refs_2_, ...), custom_call_target="tpu_custom_call" | custom-call | tf_op jit(solution)/shard_map/pallas_call | solution.py:160
  20.7 0.5 %collective-permute-done.5.refs_2_.refs_3_ = bf16[2048,128]{1,0:T(8,128)(2,1)S(1)} collective-permute-done((bf16[2048,128]{1,0:T(8,128)(2,1)S(1)}, bf16[2048,128]{1,0:T(8,128)(2,1)S(1)}, u32[]{:S(2)}, u32[]{:S(2)}) %collective-permute-start.5) | collective-permute-done | bytes 524320 | tf_op jit(solution)/shard_map/ppermute | solution.py:120
  21.1 1.2 %shard_map.61 = bf16[144,512]{1,0:T(8,128)(2,1)S(1)} custom-call(s32[16,512]{1,0:T(8,128)S(1)} %broadcast_subtract_fusion.refs_0_, bf16[512,128]{1,0:T(8,128)(2,1)S(1)} %collective-permute-done.3.refs_1_, bf16[2048,128]{1,0:T(8,128)(2,1)S(1)} %collective-permute-done.5.refs_2_.refs_3_, f32[1,512]{1,0:T(1,128)S(1)} %get-tuple-element.91.refs_3_, ...), custom_call_target="tpu_custom_call" | custom-call | tf_op jit(solution)/shard_map/pallas_call | solution.py:160
  22.4 2.1 %shard_map.62 = bf16[144,512]{1,0:T(8,128)(2,1)S(1)} custom-call(s32[16,512]{1,0:T(8,128)S(1)} %broadcast_subtract_fusion.refs_0_, bf16[512,128]{1,0:T(8,128)(2,1)S(1)} %collective-permute-done.2.refs_1_, bf16[2048,128]{1,0:T(8,128)(2,1)S(1)} %collective-permute-done.4.refs_2_, bf16[2048,128]{1,0:T(8,128)(2,1)S(1)} %collective-permute-done.5.refs_2_.refs_3_, ...), custom_call_target="tpu_custom_call" | custom-call | tf_op jit(solution)/shard_map/pallas_call | solution.py:160
  24.5 2.3 %shard_map.63 = bf16[144,512]{1,0:T(8,128)(2,1)S(1)} custom-call(s32[16,512]{1,0:T(8,128)S(1)} %broadcast_subtract_fusion.refs_0_, bf16[512,128]{1,0:T(8,128)(2,1)S(1)} %collective-permute-done.1.refs_1_, bf16[2048,128]{1,0:T(8,128)(2,1)S(1)} %collective-permute-done.4.refs_2_, bf16[2048,128]{1,0:T(8,128)(2,1)S(1)} %collective-permute-done.5.refs_2_.refs_3_, ...), custom_call_target="tpu_custom_call" | custom-call | tf_op jit(solution)/shard_map/pallas_call | solution.py:160
  26.8 1.1 %collective-permute-start.6 = (bf16[144,512]{1,0:T(8,128)(2,1)S(1)}, bf16[144,512]{1,0:T(8,128)(2,1)S(1)}, u32[]{:S(2)}, u32[]{:S(2)}) collective-permute-start(bf16[144,512]{1,0:T(8,128)(2,1)S(1)} %shard_map.63), channel_id=1, source_target_pairs={{0,4},{1,5},{2,6},{3,7},{4,0},{5,1},{6,2},{7,3},{8,12},{9,13},{10,... | collective-permute-start | bytes 442376 | tf_op jit(solution)/shard_map/ppermute | solution.py:120
  27.9 2.2 %collective-permute-start.7 = (bf16[144,512]{1,0:T(8,128)(2,1)S(1)}, bf16[144,512]{1,0:T(8,128)(2,1)S(1)}, u32[]{:S(2)}, u32[]{:S(2)}) collective-permute-start(bf16[144,512]{1,0:T(8,128)(2,1)S(1)} %shard_map.62), channel_id=1, source_target_pairs={{0,8},{1,9},{2,10},{3,11},{4,12},{5,13},{6,14},{7,15},{8,0},{9,1},... | collective-permute-start | bytes 442376 | tf_op jit(solution)/shard_map/ppermute | solution.py:120
  30.1 0.2 collective-permute-start.8
  30.3 2.0 %shard_map.64 = (f32[128,512]{1,0:T(8,128)S(1)}, f32[1,512]{1,0:T(1,128)S(1)}) custom-call(s32[16,512]{1,0:T(8,128)S(1)} %broadcast_subtract_fusion.refs_0_, bf16[512,128]{1,0:T(8,128)(2,1)S(1)} %bitcast.17, bf16[2048,128]{1,0:T(8,128)(2,1)S(1)} %collective-permute-done.4.refs_2_, bf16[2048,128]{1,0:T(8,128)(2,1)S(1)} %collective-permute-done.5.refs_2_.refs_3_, ...), custom_call_target="tpu_custom_call" | custom-call | tf_op jit(solution)/shard_map/pallas_call | solution.py:160
  32.4 0.0 collective-permute-done.6.refs_2_
  32.4 7.0 %collective-permute-done.7.refs_3_ = bf16[144,512]{1,0:T(8,128)(2,1)S(1)} collective-permute-done((bf16[144,512]{1,0:T(8,128)(2,1)S(1)}, bf16[144,512]{1,0:T(8,128)(2,1)S(1)}, u32[]{:S(2)}, u32[]{:S(2)}) %collective-permute-start.7) | collective-permute-done | bytes 147488 | tf_op jit(solution)/shard_map/ppermute | solution.py:120
  39.3 4.1 %collective-permute-done.8.refs_4_ = bf16[144,512]{1,0:T(8,128)(2,1)S(1)} collective-permute-done((bf16[144,512]{1,0:T(8,128)(2,1)S(1)}, bf16[144,512]{1,0:T(8,128)(2,1)S(1)}, u32[]{:S(2)}, u32[]{:S(2)}) %collective-permute-start.8) | collective-permute-done | bytes 147488 | tf_op jit(solution)/shard_map/ppermute | solution.py:120
  43.4 1.0 %merge.1 = bf16[512,128]{1,0:T(8,128)(2,1)} custom-call(f32[128,512]{1,0:T(8,128)S(1)} %get-tuple-element.108.refs_0_, f32[1,512]{1,0:T(1,128)S(1)} %get-tuple-element.109.refs_1_, bf16[144,512]{1,0:T(8,128)(2,1)S(1)} %collective-permute-done.6.refs_2_, bf16[144,512]{1,0:T(8,128)(2,1)S(1)} %collective-permute-done.7.refs_3_, ...), custom_call_target="tpu_custom_call" | custom-call | tf_op jit(solution)/shard_map/merge/pallas_call | solution.py:198
  (8 shorter events, 0.1 us)
Async XLA Ops:
  0.0 3.6 %copy-start.1 = (bf16[1024,128]{1,0:T(8,128)(2,1)S(1)}, bf16[1024,128]{1,0:T(8,128)(2,1)}, u32[]{:S(2)}) copy-start(bf16[1024,128]{1,0:T(8,128)(2,1)} %param.7) | copy-start | bytes 786436
  0.0 9.4 %collective-permute-start.1 = (bf16[512,128]{1,0:T(8,128)(2,1)}, bf16[512,128]{1,0:T(8,128)(2,1)S(1)}, u32[]{:S(2)}, u32[]{:S(2)}) collective-permute-start(bf16[512,128]{1,0:T(8,128)(2,1)} %bitcast.12), channel_id=1, source_target_pairs={{0,4},{1,5},{2,6},{3,7},{4,0},{5,1},{6,2},{7,3},{8,12},{9,13},{10,... | collective-permute-start | bytes 393224 | tf_op jit(solution)/shard_map/ppermute | solution.py:120
  0.2 11.3 %collective-permute-start.2 = (bf16[512,128]{1,0:T(8,128)(2,1)}, bf16[512,128]{1,0:T(8,128)(2,1)S(1)}, u32[]{:S(2)}, u32[]{:S(2)}) collective-permute-start(bf16[512,128]{1,0:T(8,128)(2,1)} %bitcast.13), channel_id=1, source_target_pairs={{0,8},{1,9},{2,10},{3,11},{4,12},{5,13},{6,14},{7,15},{8,0},{9,1},... | collective-permute-start | bytes 393224 | tf_op jit(solution)/shard_map/ppermute | solution.py:120
  2.5 11.6 %collective-permute-start.3 = (bf16[512,128]{1,0:T(8,128)(2,1)}, bf16[512,128]{1,0:T(8,128)(2,1)S(1)}, u32[]{:S(2)}, u32[]{:S(2)}) collective-permute-start(bf16[512,128]{1,0:T(8,128)(2,1)} %bitcast.14), channel_id=1, source_target_pairs={{0,12},{1,13},{2,14},{3,15},{4,8},{5,9},{6,10},{7,11},{8,4},{9,5},... | collective-permute-start | bytes 393224 | tf_op jit(solution)/shard_map/ppermute | solution.py:120
  3.7 4.7 %collective-permute-start = (bf16[2048,128]{1,0:T(8,128)(2,1)S(1)}, bf16[2048,128]{1,0:T(8,128)(2,1)S(1)}, u32[]{:S(2)}, u32[]{:S(2)}) collective-permute-start(bf16[2048,128]{1,0:T(8,128)(2,1)S(1)} %constant_dynamic-update-slice_fusion.refs_2_), channel_id=1, source_target_pairs={{0,1},{1,0},{2,3},{3,2},{4,5},{5,4},{6,7},{7,6},{8,9},{9,8},{10,11... | collective-permute-start | bytes 1572872 | tf_op jit(solution)/shard_map/ppermute | solution.py:120
  5.3 13.4 %collective-permute-start.4 = (bf16[2048,128]{1,0:T(8,128)(2,1)S(1)}, bf16[2048,128]{1,0:T(8,128)(2,1)S(1)}, u32[]{:S(2)}, u32[]{:S(2)}) collective-permute-start(bf16[2048,128]{1,0:T(8,128)(2,1)S(1)} %constant_dynamic-update-slice_fusion.refs_2_), channel_id=1, source_target_pairs={{0,2},{1,3},{2,0},{3,1},{4,6},{5,7},{6,4},{7,5},{8,10},{9,11},{10,... | collective-permute-start | bytes 1572872 | tf_op jit(solution)/shard_map/ppermute | solution.py:120
  5.5 0.7 %copy-start.2 = (s32[512]{0:T(512)S(1)}, s32[512]{0:T(512)}, u32[]{:S(2)}) copy-start(s32[512]{0:T(512)} %param.9) | copy-start | bytes 6148
  6.4 0.9 %copy-start = (bf16[32,16,128]{2,1,0:T(8,128)(2,1)S(1)}, bf16[32,16,128]{2,1,0:T(8,128)(2,1)}, u32[]{:S(2)}) copy-start(bf16[32,16,128]{2,1,0:T(8,128)(2,1)} %param.5) | copy-start | bytes 393220
  18.7 2.5 %collective-permute-start.5 = (bf16[2048,128]{1,0:T(8,128)(2,1)S(1)}, bf16[2048,128]{1,0:T(8,128)(2,1)S(1)}, u32[]{:S(2)}, u32[]{:S(2)}) collective-permute-start(bf16[2048,128]{1,0:T(8,128)(2,1)S(1)} %collective-permute-done.4.refs_2_), channel_id=1, source_target_pairs={{0,1},{1,0},{2,3},{3,2},{4,5},{5,4},{6,7},{7,6},{8,9},{9,8},{10,11... | collective-permute-start | bytes 1572872 | tf_op jit(solution)/shard_map/ppermute | solution.py:120
  26.8 5.6 %collective-permute-start.6 = (bf16[144,512]{1,0:T(8,128)(2,1)S(1)}, bf16[144,512]{1,0:T(8,128)(2,1)S(1)}, u32[]{:S(2)}, u32[]{:S(2)}) collective-permute-start(bf16[144,512]{1,0:T(8,128)(2,1)S(1)} %shard_map.63), channel_id=1, source_target_pairs={{0,4},{1,5},{2,6},{3,7},{4,0},{5,1},{6,2},{7,3},{8,12},{9,13},{10,... | collective-permute-start | bytes 442376 | tf_op jit(solution)/shard_map/ppermute | solution.py:120
  27.9 11.4 %collective-permute-start.7 = (bf16[144,512]{1,0:T(8,128)(2,1)S(1)}, bf16[144,512]{1,0:T(8,128)(2,1)S(1)}, u32[]{:S(2)}, u32[]{:S(2)}) collective-permute-start(bf16[144,512]{1,0:T(8,128)(2,1)S(1)} %shard_map.62), channel_id=1, source_target_pairs={{0,8},{1,9},{2,10},{3,11},{4,12},{5,13},{6,14},{7,15},{8,0},{9,1},... | collective-permute-start | bytes 442376 | tf_op jit(solution)/shard_map/ppermute | solution.py:120
  30.1 13.3 %collective-permute-start.8 = (bf16[144,512]{1,0:T(8,128)(2,1)S(1)}, bf16[144,512]{1,0:T(8,128)(2,1)S(1)}, u32[]{:S(2)}, u32[]{:S(2)}) collective-permute-start(bf16[144,512]{1,0:T(8,128)(2,1)S(1)} %shard_map.61), channel_id=1, source_target_pairs={{0,12},{1,13},{2,14},{3,15},{4,8},{5,9},{6,10},{7,11},{8,4},{9,5},... | collective-permute-start | bytes 442376 | tf_op jit(solution)/shard_map/ppermute | solution.py:120
where the time goes:
time: 45.4 us; the launch traced here: 44.5 us
  Pallas kernels  17.9 us (39%)
  waiting for transfers between devices  14.7 us (32%)
  starting transfers between devices  8.94 us (20%)
  local copies, waits for them, and re-layouts  1.99 us (4%)
  between operations  0.84 us (2%)
    pallas_call x10, Pallas kernels, attend(): pl.pallas_call(functools.partial(attend_kernel, scale, [index * inner + b...  16.8 us
    ppermute x9, waiting for transfers between devices, swap(): return lax.ppermute(array, 'ctx', [(i, i ^ step) for i in range(size)])  14.7 us
    ppermute x9, starting transfers between devices, swap(): return lax.ppermute(array, 'ctx', [(i, i ^ step) for i in range(size)])  8.94 us
    unnamed x7, local copies, waits for them, and re-layouts  1.58 us
    pallas_call x1, Pallas kernels, local(): pl.pallas_call(functools.partial(merge_kernel, outer), in_specs=[vmem] *...  1.03 us
  transfers between devices with their start and end apart: 9, of which 5 were waited for; matrix products, arithmetic and copies ran while one was open for 3% of the time, Pallas kernels for 25%

commit v1 on v0

--- a/solution.py
+++ b/solution.py
@@ -59,18 +59,16 @@
 
 def attend_kernel(scale, rows_of, has_state, form, own_rows, *refs):
     limits_ref, q_ref = refs[:2]
-    pair_refs = refs[2 : 2 + len(rows_of)]
-    rest = refs[2 + len(rows_of) :]
+    pair_refs = refs[2 : 2 + 2 * len(rows_of)]
+    rest = refs[2 + 2 * len(rows_of) :]
     query = q_ref[...]
     state = None
     if has_state:
         state = tuple(ref[...] for ref in rest[:3])
         rest = rest[3:]
-    for row, pair_ref in zip(rows_of, pair_refs):
-        shard_keys = pair_ref.shape[0] // 2
-        state = block_update(
-            state, query, pair_ref[:shard_keys, :], pair_ref[shard_keys:, :], limits_ref[row : row + 1, :], scale
-        )
+    for at, row in enumerate(rows_of):
+        keys, values = pair_refs[2 * at][...], pair_refs[2 * at + 1][...]
+        state = block_update(state, query, keys, values, limits_ref[row : row + 1, :], scale)
     if form == "state":
         for ref, value in zip(rest, state):
             ref[...] = value
@@ -120,13 +118,20 @@
         return lax.ppermute(array, "ctx", [(i, i ^ step) for i in range(size)])
 
     query = queries.reshape(rows, head_width)
-    own_pair = jnp.concatenate([cache_keys, cache_values], axis=0)
-    far_pair = swap(own_pair, 2)
-    got = [query] + [swap(query, inner * k) for k in range(1, outer)]
-    near_pair = swap(own_pair, 1)
-
     per_stage = max(outer // 4, 1)
     stages = [list(range(s, s + per_stage)) for s in range(0, outer, per_stage)]
+    last = len(stages) - 1
+
+    far_pair = [swap(cache_keys, 2), swap(cache_values, 2)]
+    near_pair = [swap(cache_keys, 1), swap(cache_values, 1)]
+    got = [query] + [None] * (outer - 1)
+
+    def gather(index):
+        for k in stages[index]:
+            if k:
+                low = k & -k
+                got[k] = swap(got[k ^ low], inner * low)
+
     stage_rows = rows * per_stage
 
     limits = (span_offset[0] + positions).reshape(outer, inner, own_tokens)
@@ -141,8 +146,7 @@
 
     vmem = pl.BlockSpec(memory_space=pltpu.VMEM)
     params = pltpu.CompilerParams(vmem_limit_bytes=40 << 20)
-    pairs = [own_pair, near_pair]
-    stage_query = [join([got[k] for k in stage], 0) for stage in stages]
+    pairs = [[cache_keys, cache_values], near_pair]
     stat = jax.ShapeDtypeStruct((1, stage_rows), jnp.float32)
     state_shapes = [stat, stat, jax.ShapeDtypeStruct((head_width, stage_rows), jnp.float32)]
     packed_shape = jax.ShapeDtypeStruct((head_width + extra_rows, stage_rows), jnp.bfloat16)
@@ -156,7 +160,7 @@
             shapes = state_shapes
         else:
             shapes = (own_shapes if own_rows else []) + ([packed_shape] if index or per_stage > 1 else [])
-        operands = [chain[0], stage_query[index]] + [pairs[b] for b in blocks] + list(states[index] or ())
+        operands = [chain[0], stage_query[index]] + [array for b in blocks for array in pairs[b]] + list(states[index] or ())
         results = pl.pallas_call(
             functools.partial(
                 attend_kernel, scale, [index * inner + b for b in blocks], states[index] is not None, form, own_rows
@@ -171,14 +175,30 @@
             states[index] = results
         return results
 
+    def hold(*arrays):
+        chain[0], arrays = lax.optimization_barrier((chain[0], arrays))
+        return list(arrays)
+
+    stage_query = [None] * len(stages)
+
+    def ready(index):
+        stage_query[index] = join([got[k] for k in stages[index]], 0)
+
+    for index in range(len(stages) - 1):
+        gather(index)
+        ready(index)
     attend(0, [0], "state")
     attend(0, [1], "state")
-    for index in range(1, len(stages)):
+    for index in range(1, last):
+        if index == last - 1:
+            source = stages[index][0]
+            (got[source],) = hold(got[source])
+            gather(last)
+            ready(last)
         attend(index, [0, 1], "state")
-
-    chain[0], far_pair = lax.optimization_barrier((chain[0], far_pair))
-    across_pair = swap(far_pair, 1)
-    pairs += [far_pair, across_pair]
+    far_pair = hold(*far_pair)
+    pairs += [far_pair, [swap(array, 1) for array in far_pair]]
+    attend(last, [0, 1], "state")
     parts = [None] * outer
 
     def send(index, packed):
@@ -187,10 +207,7 @@
                 piece = packed if per_stage == 1 else packed[:, at * rows : (at + 1) * rows]
                 parts[k] = swap(piece, inner * k)
 
-    last = len(stages) - 1
-    attend(last, [2], "state")
-    send(last, attend(last, [3], "packed")[0])
-    for index in range(last - 1, 0, -1):
+    for index in [last - 1, last] + list(range(last - 2, 0, -1)):
         send(index, attend(index, [2, 3], "packed")[0])
     results = attend(0, [2, 3], "packed")
     if per_stage > 1:

time: 45.4 us -> 51 us (1.12)
  the two profiles are of different devices: /device:TPU:13 before, /device:TPU:0 now
where the time goes in v1:
time: 51 us; the launch traced here: 50.8 us
  waiting for transfers between devices  18 us (35%)
  Pallas kernels  17.8 us (35%)
  starting transfers between devices  12.1 us (24%)
  local copies, waits for them, and re-layouts  1.33 us (3%)
  between operations  0.85 us (2%)
  other arithmetic  0.77 us (2%)
    ppermute x12, waiting for transfers between devices, swap(): return lax.ppermute(array, 'ctx', [(i, i ^ step) for i in range(size)])  18 us
    pallas_call x9, Pallas kernels, attend(): pl.pallas_call(functools.partial(attend_kernel, scale, [index * inner + b...  16.7 us
    ppermute x12, starting transfers between devices, swap(): return lax.ppermute(array, 'ctx', [(i, i ^ step) for i in range(size)])  12.1 us
    pallas_call x1, Pallas kernels, local(): pl.pallas_call(functools.partial(merge_kernel, outer), in_specs=[vmem] *...  1.03 us
  transfers between devices with their start and end apart: 12, of which 5 were waited for; matrix products, arithmetic and copies ran while one was open for 2% of the time, Pallas kernels for 20%

profile of v1, /device:TPU:0, one launch (start us, length us, event | category | flops | bytes accessed | tf_op | source)
XLA Modules:
  0.0 50.8 jit_solution(7700491077390042192)
XLA Ops:
  0.0 0.0 copy-start
  0.0 0.5 collective-permute-start
  0.5 2.6 %collective-permute-start.4 = (bf16[1024,128]{1,0:T(8,128)(2,1)}, bf16[1024,128]{1,0:T(8,128)(2,1)S(1)}, u32[]{:S(2)}, u32[]{:S(2)}) collective-permute-start(bf16[1024,128]{1,0:T(8,128)(2,1)} %refs_2_.7), channel_id=1, source_target_pairs={{0,2},{1,3},{2,0},{3,1},{4,6},{5,7},{6,4},{7,5},{8,10},{9,11},{10,... | collective-permute-start | bytes 786440 | tf_op jit(solution)/shard_map/ppermute | solution.py:118
  3.1 0.2 collective-permute-start.1
  3.2 0.3 collective-permute-start.5
  3.5 2.8 %collective-permute-start.3 = (bf16[512,128]{1,0:T(8,128)(2,1)}, bf16[512,128]{1,0:T(8,128)(2,1)S(1)}, u32[]{:S(2)}, u32[]{:S(2)}) collective-permute-start(bf16[512,128]{1,0:T(8,128)(2,1)} %bitcast.12), channel_id=1, source_target_pairs={{0,8},{1,9},{2,10},{3,11},{4,12},{5,13},{6,14},{7,15},{8,0},{9,1},... | collective-permute-start | bytes 393224 | tf_op jit(solution)/shard_map/ppermute | solution.py:118
  7.0 0.7 %broadcast_add_fusion = s32[512]{0:T(512)S(1)} fusion(s32[512]{0:T(512)} %param.9, s32[]{:T(128)} %bitcast.11), kind=kLoop, calls=%fused_computation.6 | loop fusion | flops 512 | bytes 4100 | tf_op jit(solution)/shard_map/add | solution.py:137
  7.7 0.1 reshape.22
  7.8 0.1 sub.31
  7.9 0.1 broadcast_in_dim.4
  8.0 0.0 copy-start.3
  8.0 0.1 sub.27
  8.1 0.0 collective-permute-done.refs_2_.refs_4_
  8.1 1.6 %collective-permute-start.2 = (bf16[512,128]{1,0:T(8,128)(2,1)}, bf16[512,128]{1,0:T(8,128)(2,1)S(1)}, u32[]{:S(2)}, u32[]{:S(2)}) collective-permute-start(bf16[512,128]{1,0:T(8,128)(2,1)} %bitcast.13), channel_id=1, source_target_pairs={{0,4},{1,5},{2,6},{3,7},{4,0},{5,1},{6,2},{7,3},{8,12},{9,13},{10,... | collective-permute-start | bytes 393224 | tf_op jit(solution)/shard_map/ppermute | solution.py:118
  9.8 0.1 broadcast_subtract_fusion.refs_0_
  9.8 0.0 copy-done
  9.8 0.0 copy-done.3
  9.8 0.0 copy-start.1
  9.8 0.9 %copy-done.1 = bf16[1024,128]{1,0:T(8,128)(2,1)S(1)} copy-done((bf16[1024,128]{1,0:T(8,128)(2,1)S(1)}, bf16[1024,128]{1,0:T(8,128)(2,1)}, u32[]{:S(2)}) %copy-start.1) | copy-done | bytes 262168
  10.8 1.1 %shard_map.55 = (f32[1,512]{1,0:T(1,128)S(1)}, f32[1,512]{1,0:T(1,128)S(1)}, f32[128,512]{1,0:T(8,128)S(1)}) custom-call(s32[16,512]{1,0:T(8,128)S(1)} %broadcast_subtract_fusion.refs_0_, bf16[512,128]{1,0:T(8,128)(2,1)S(1)} %bitcast.14, bf16[1024,128]{1,0:T(8,128)(2,1)S(1)} %copy-done, bf16[1024,128]{1,0:T(8,128)(2,1)S(1)} %copy-done.1), custom_call_target="tpu_custom_call" | custom-call | tf_op jit(solution)/shard_map/pallas_call | solution.py:164
  11.9 0.0 copy-start.2
  11.9 0.0 collective-permute-done.1.refs_3_.refs_5_
  11.9 1.1 %shard_map.56 = (f32[1,512]{1,0:T(1,128)S(1)}, f32[1,512]{1,0:T(1,128)S(1)}, f32[128,512]{1,0:T(8,128)S(1)}) custom-call(s32[16,512]{1,0:T(8,128)S(1)} %broadcast_subtract_fusion.refs_0_, bf16[512,128]{1,0:T(8,128)(2,1)S(1)} %bitcast.15, bf16[1024,128]{1,0:T(8,128)(2,1)S(1)} %collective-permute-done.refs_2_.refs_4_, ...), custom_call_target="tpu_custom_call" | custom-call | tf_op jit(solution)/shard_map/pallas_call | solution.py:164
  13.0 2.2 %collective-permute-done.2.refs_1_ = bf16[512,128]{1,0:T(8,128)(2,1)S(1)} collective-permute-done((bf16[512,128]{1,0:T(8,128)(2,1)}, bf16[512,128]{1,0:T(8,128)(2,1)S(1)}, u32[]{:S(2)}, u32[]{:S(2)}) %collective-permute-start.2) | collective-permute-done | bytes 131104 | tf_op jit(solution)/shard_map/ppermute | solution.py:118
  15.1 0.0 copy-done.2
  15.1 2.0 %shard_map.57 = (f32[1,512]{1,0:T(1,128)S(1)}, f32[1,512]{1,0:T(1,128)S(1)}, f32[128,512]{1,0:T(8,128)S(1)}) custom-call(s32[16,512]{1,0:T(8,128)S(1)} %broadcast_subtract_fusion.refs_0_, bf16[512,128]{1,0:T(8,128)(2,1)S(1)} %collective-permute-done.2.refs_1_, bf16[1024,128]{1,0:T(8,128)(2,1)S(1)} %copy-done, bf16[1024,128]{1,0:T(8,128)(2,1)S(1)} %copy-done.2, ...), custom_call_target="tpu_custom_call" | custom-call | tf_op jit(solution)/shard_map/pallas_call | solution.py:164
  17.1 0.0 collective-permute-done.3.refs_1_
  17.1 2.0 %shard_map.58 = (f32[1,512]{1,0:T(1,128)S(1)}, f32[1,512]{1,0:T(1,128)S(1)}, f32[128,512]{1,0:T(8,128)S(1)}) custom-call(s32[16,512]{1,0:T(8,128)S(1)} %broadcast_subtract_fusion.refs_0_, bf16[512,128]{1,0:T(8,128)(2,1)S(1)} %collective-permute-done.3.refs_1_, bf16[1024,128]{1,0:T(8,128)(2,1)S(1)} %copy-done, bf16[1024,128]{1,0:T(8,128)(2,1)S(1)} %copy-done.2, ...), custom_call_target="tpu_custom_call" | custom-call | tf_op jit(solution)/shard_map/pallas_call | solution.py:164
  19.1 0.0 collective-permute-done.4.refs_2_
  19.1 0.0 collective-permute-done.5.refs_3_
  19.2 0.1 collective-permute-start.7
  19.2 0.5 collective-permute-start.8
  19.7 0.0 collective-permute-start.6
  19.7 5.5 %collective-permute-done.6.refs_1_ = bf16[512,128]{1,0:T(8,128)(2,1)S(1)} collective-permute-done((bf16[512,128]{1,0:T(8,128)(2,1)S(1)}, bf16[512,128]{1,0:T(8,128)(2,1)S(1)}, u32[]{:S(2)}, u32[]{:S(2)}) %collective-permute-start.6) | collective-permute-done | bytes 131104 | tf_op jit(solution)/shard_map/ppermute | solution.py:118
  25.2 2.0 %shard_map.59 = (f32[1,512]{1,0:T(1,128)S(1)}, f32[1,512]{1,0:T(1,128)S(1)}, f32[128,512]{1,0:T(8,128)S(1)}) custom-call(s32[16,512]{1,0:T(8,128)S(1)} %broadcast_subtract_fusion.refs_0_, bf16[512,128]{1,0:T(8,128)(2,1)S(1)} %collective-permute-done.6.refs_1_, bf16[1024,128]{1,0:T(8,128)(2,1)S(1)} %copy-done, bf16[1024,128]{1,0:T(8,128)(2,1)S(1)} %copy-done.2, ...), custom_call_target="tpu_custom_call" | custom-call | tf_op jit(solution)/shard_map/pallas_call | solution.py:164
  27.2 0.0 collective-permute-done.7.refs_4_
  27.2 0.0 collective-permute-done.8.refs_5_
  27.2 2.1 %shard_map.60 = bf16[144,512]{1,0:T(8,128)(2,1)S(1)} custom-call(s32[16,512]{1,0:T(8,128)S(1)} %broadcast_subtract_fusion.refs_0_, bf16[512,128]{1,0:T(8,128)(2,1)S(1)} %collective-permute-done.3.refs_1_, bf16[1024,128]{1,0:T(8,128)(2,1)S(1)} %collective-permute-done.4.refs_2_, bf16[1024,128]{1,0:T(8,128)(2,1)S(1)} %collective-permute-done.5.refs_3_, ...), custom_call_target="tpu_custom_call" | custom-call | tf_op jit(solution)/shard_map/pallas_call | solution.py:164
  29.4 2.1 %shard_map.61 = bf16[144,512]{1,0:T(8,128)(2,1)S(1)} custom-call(s32[16,512]{1,0:T(8,128)S(1)} %broadcast_subtract_fusion.refs_0_, bf16[512,128]{1,0:T(8,128)(2,1)S(1)} %collective-permute-done.6.refs_1_, bf16[1024,128]{1,0:T(8,128)(2,1)S(1)} %collective-permute-done.4.refs_2_, bf16[1024,128]{1,0:T(8,128)(2,1)S(1)} %collective-permute-done.5.refs_3_, ...), custom_call_target="tpu_custom_call" | custom-call | tf_op jit(solution)/shard_map/pallas_call | solution.py:164
  31.5 2.3 %shard_map.62 = bf16[144,512]{1,0:T(8,128)(2,1)S(1)} custom-call(s32[16,512]{1,0:T(8,128)S(1)} %broadcast_subtract_fusion.refs_0_, bf16[512,128]{1,0:T(8,128)(2,1)S(1)} %collective-permute-done.2.refs_1_, bf16[1024,128]{1,0:T(8,128)(2,1)S(1)} %collective-permute-done.4.refs_2_, bf16[1024,128]{1,0:T(8,128)(2,1)S(1)} %collective-permute-done.5.refs_3_, ...), custom_call_target="tpu_custom_call" | custom-call | tf_op jit(solution)/shard_map/pallas_call | solution.py:164
  33.9 0.4 collective-permute-start.9
  34.2 2.5 %collective-permute-start.11 = (bf16[144,512]{1,0:T(8,128)(2,1)S(1)}, bf16[144,512]{1,0:T(8,128)(2,1)S(1)}, u32[]{:S(2)}, u32[]{:S(2)}) collective-permute-start(bf16[144,512]{1,0:T(8,128)(2,1)S(1)} %shard_map.61), channel_id=1, source_target_pairs={{0,12},{1,13},{2,14},{3,15},{4,8},{5,9},{6,10},{7,11},{8,4},{9,5},... | collective-permute-start | bytes 442376 | tf_op jit(solution)/shard_map/ppermute | solution.py:118
  36.7 0.7 %collective-permute-start.10 = (bf16[144,512]{1,0:T(8,128)(2,1)S(1)}, bf16[144,512]{1,0:T(8,128)(2,1)S(1)}, u32[]{:S(2)}, u32[]{:S(2)}) collective-permute-start(bf16[144,512]{1,0:T(8,128)(2,1)S(1)} %shard_map.60), channel_id=1, source_target_pairs={{0,8},{1,9},{2,10},{3,11},{4,12},{5,13},{6,14},{7,15},{8,0},{9,1},... | collective-permute-start | bytes 442376 | tf_op jit(solution)/shard_map/ppermute | solution.py:118
  37.4 2.0 %shard_map.63 = (f32[128,512]{1,0:T(8,128)S(1)}, f32[1,512]{1,0:T(1,128)S(1)}) custom-call(s32[16,512]{1,0:T(8,128)S(1)} %broadcast_subtract_fusion.refs_0_, bf16[512,128]{1,0:T(8,128)(2,1)S(1)} %bitcast.16, bf16[1024,128]{1,0:T(8,128)(2,1)S(1)} %collective-permute-done.4.refs_2_, bf16[1024,128]{1,0:T(8,128)(2,1)S(1)} %collective-permute-done.5.refs_3_, ...), custom_call_target="tpu_custom_call" | custom-call | tf_op jit(solution)/shard_map/pallas_call | solution.py:164
  39.4 0.7 %collective-permute-done.9.refs_2_ = bf16[144,512]{1,0:T(8,128)(2,1)S(1)} collective-permute-done((bf16[144,512]{1,0:T(8,128)(2,1)S(1)}, bf16[144,512]{1,0:T(8,128)(2,1)S(1)}, u32[]{:S(2)}, u32[]{:S(2)}) %collective-permute-start.9) | collective-permute-done | bytes 147488 | tf_op jit(solution)/shard_map/ppermute | solution.py:118
  40.1 4.5 %collective-permute-done.11.refs_4_ = bf16[144,512]{1,0:T(8,128)(2,1)S(1)} collective-permute-done((bf16[144,512]{1,0:T(8,128)(2,1)S(1)}, bf16[144,512]{1,0:T(8,128)(2,1)S(1)}, u32[]{:S(2)}, u32[]{:S(2)}) %collective-permute-start.11) | collective-permute-done | bytes 147488 | tf_op jit(solution)/shard_map/ppermute | solution.py:118
  44.7 5.1 %collective-permute-done.10.refs_3_ = bf16[144,512]{1,0:T(8,128)(2,1)S(1)} collective-permute-done((bf16[144,512]{1,0:T(8,128)(2,1)S(1)}, bf16[144,512]{1,0:T(8,128)(2,1)S(1)}, u32[]{:S(2)}, u32[]{:S(2)}) %collective-permute-start.10) | collective-permute-done | bytes 147488 | tf_op jit(solution)/shard_map/ppermute | solution.py:118
  49.8 1.0 %merge.1 = bf16[512,128]{1,0:T(8,128)(2,1)} custom-call(f32[128,512]{1,0:T(8,128)S(1)} %get-tuple-element.100.refs_0_, f32[1,512]{1,0:T(1,128)S(1)} %get-tuple-element.101.refs_1_, bf16[144,512]{1,0:T(8,128)(2,1)S(1)} %collective-permute-done.9.refs_2_, bf16[144,512]{1,0:T(8,128)(2,1)S(1)} %collective-permute-done.10.refs_3_, ...), custom_call_target="tpu_custom_call" | custom-call | tf_op jit(solution)/shard_map/merge/pallas_call | solution.py:215
  (6 shorter events, 0.1 us)
Async XLA Ops:
  0.0 9.8 %copy-start = (bf16[1024,128]{1,0:T(8,128)(2,1)S(1)}, bf16[1024,128]{1,0:T(8,128)(2,1)}, u32[]{:S(2)}) copy-start(bf16[1024,128]{1,0:T(8,128)(2,1)} %refs_2_.7) | copy-start | bytes 786436
  0.0 8.1 %collective-permute-start = (bf16[1024,128]{1,0:T(8,128)(2,1)}, bf16[1024,128]{1,0:T(8,128)(2,1)S(1)}, u32[]{:S(2)}, u32[]{:S(2)}) collective-permute-start(bf16[1024,128]{1,0:T(8,128)(2,1)} %refs_2_.7), channel_id=1, source_target_pairs={{0,1},{1,0},{2,3},{3,2},{4,5},{5,4},{6,7},{7,6},{8,9},{9,8},{10,11... | collective-permute-start | bytes 786440 | tf_op jit(solution)/shard_map/ppermute | solution.py:118
  0.5 18.6 %collective-permute-start.4 = (bf16[1024,128]{1,0:T(8,128)(2,1)}, bf16[1024,128]{1,0:T(8,128)(2,1)S(1)}, u32[]{:S(2)}, u32[]{:S(2)}) collective-permute-start(bf16[1024,128]{1,0:T(8,128)(2,1)} %refs_2_.7), channel_id=1, source_target_pairs={{0,2},{1,3},{2,0},{3,1},{4,6},{5,7},{6,4},{7,5},{8,10},{9,11},{10,... | collective-permute-start | bytes 786440 | tf_op jit(solution)/shard_map/ppermute | solution.py:118
  3.1 8.8 %collective-permute-start.1 = (bf16[1024,128]{1,0:T(8,128)(2,1)}, bf16[1024,128]{1,0:T(8,128)(2,1)S(1)}, u32[]{:S(2)}, u32[]{:S(2)}) collective-permute-start(bf16[1024,128]{1,0:T(8,128)(2,1)} %refs_3_.7), channel_id=1, source_target_pairs={{0,1},{1,0},{2,3},{3,2},{4,5},{5,4},{6,7},{7,6},{8,9},{9,8},{10,11... | collective-permute-start | bytes 786440 | tf_op jit(solution)/shard_map/ppermute | solution.py:118
  3.2 15.9 %collective-permute-start.5 = (bf16[1024,128]{1,0:T(8,128)(2,1)}, bf16[1024,128]{1,0:T(8,128)(2,1)S(1)}, u32[]{:S(2)}, u32[]{:S(2)}) collective-permute-start(bf16[1024,128]{1,0:T(8,128)(2,1)} %refs_3_.7), channel_id=1, source_target_pairs={{0,2},{1,3},{2,0},{3,1},{4,6},{5,7},{6,4},{7,5},{8,10},{9,11},{10,... | collective-permute-start | bytes 786440 | tf_op jit(solution)/shard_map/ppermute | solution.py:118
  3.5 13.6 %collective-permute-start.3 = (bf16[512,128]{1,0:T(8,128)(2,1)}, bf16[512,128]{1,0:T(8,128)(2,1)S(1)}, u32[]{:S(2)}, u32[]{:S(2)}) collective-permute-start(bf16[512,128]{1,0:T(8,128)(2,1)} %bitcast.12), channel_id=1, source_target_pairs={{0,8},{1,9},{2,10},{3,11},{4,12},{5,13},{6,14},{7,15},{8,0},{9,1},... | collective-permute-start | bytes 393224 | tf_op jit(solution)/shard_map/ppermute | solution.py:118
  8.0 1.9 %copy-start.3 = (bf16[32,16,128]{2,1,0:T(8,128)(2,1)S(1)}, bf16[32,16,128]{2,1,0:T(8,128)(2,1)}, u32[]{:S(2)}) copy-start(bf16[32,16,128]{2,1,0:T(8,128)(2,1)} %param.5) | copy-start | bytes 393220
  8.1 7.0 %collective-permute-start.2 = (bf16[512,128]{1,0:T(8,128)(2,1)}, bf16[512,128]{1,0:T(8,128)(2,1)S(1)}, u32[]{:S(2)}, u32[]{:S(2)}) collective-permute-start(bf16[512,128]{1,0:T(8,128)(2,1)} %bitcast.13), channel_id=1, source_target_pairs={{0,4},{1,5},{2,6},{3,7},{4,0},{5,1},{6,2},{7,3},{8,12},{9,13},{10,... | collective-permute-start | bytes 393224 | tf_op jit(solution)/shard_map/ppermute | solution.py:118
  9.8 1.0 %copy-start.1 = (bf16[1024,128]{1,0:T(8,128)(2,1)S(1)}, bf16[1024,128]{1,0:T(8,128)(2,1)}, u32[]{:S(2)}) copy-start(bf16[1024,128]{1,0:T(8,128)(2,1)} %refs_3_.7) | copy-start | bytes 786436
  11.9 3.3 %copy-start.2 = (bf16[1024,128]{1,0:T(8,128)(2,1)S(1)}, bf16[1024,128]{1,0:T(8,128)(2,1)}, u32[]{:S(2)}) copy-start(bf16[1024,128]{1,0:T(8,128)(2,1)} %refs_3_.7) | copy-start | bytes 786436
  19.2 8.1 %collective-permute-start.7 = (bf16[1024,128]{1,0:T(8,128)(2,1)S(1)}, bf16[1024,128]{1,0:T(8,128)(2,1)S(1)}, u32[]{:S(2)}, u32[]{:S(2)}) collective-permute-start(bf16[1024,128]{1,0:T(8,128)(2,1)S(1)} %collective-permute-done.4.refs_2_), channel_id=1, source_target_pairs={{0,1},{1,0},{2,3},{3,2},{4,5},{5,4},{6,7},{7,6},{8,9},{9,8},{10,11... | collective-permute-start | bytes 786440 | tf_op jit(solution)/shard_map/ppermute | solution.py:118
  19.2 8.0 %collective-permute-start.8 = (bf16[1024,128]{1,0:T(8,128)(2,1)S(1)}, bf16[1024,128]{1,0:T(8,128)(2,1)S(1)}, u32[]{:S(2)}, u32[]{:S(2)}) collective-permute-start(bf16[1024,128]{1,0:T(8,128)(2,1)S(1)} %collective-permute-done.5.refs_3_), channel_id=1, source_target_pairs={{0,1},{1,0},{2,3},{3,2},{4,5},{5,4},{6,7},{7,6},{8,9},{9,8},{10,11... | collective-permute-start | bytes 786440 | tf_op jit(solution)/shard_map/ppermute | solution.py:118
  19.7 5.5 %collective-permute-start.6 = (bf16[512,128]{1,0:T(8,128)(2,1)S(1)}, bf16[512,128]{1,0:T(8,128)(2,1)S(1)}, u32[]{:S(2)}, u32[]{:S(2)}) collective-permute-start(bf16[512,128]{1,0:T(8,128)(2,1)S(1)} %collective-permute-done.3.refs_1_), channel_id=1, source_target_pairs={{0,4},{1,5},{2,6},{3,7},{4,0},{5,1},{6,2},{7,3},{8,12},{9,13},{10,... | collective-permute-start | bytes 393224 | tf_op jit(solution)/shard_map/ppermute | solution.py:118
  33.9 6.3 %collective-permute-start.9 = (bf16[144,512]{1,0:T(8,128)(2,1)S(1)}, bf16[144,512]{1,0:T(8,128)(2,1)S(1)}, u32[]{:S(2)}, u32[]{:S(2)}) collective-permute-start(bf16[144,512]{1,0:T(8,128)(2,1)S(1)} %shard_map.62), channel_id=1, source_target_pairs={{0,4},{1,5},{2,6},{3,7},{4,0},{5,1},{6,2},{7,3},{8,12},{9,13},{10,... | collective-permute-start | bytes 442376 | tf_op jit(solution)/shard_map/ppermute | solution.py:118
  34.2 10.4 %collective-permute-start.11 = (bf16[144,512]{1,0:T(8,128)(2,1)S(1)}, bf16[144,512]{1,0:T(8,128)(2,1)S(1)}, u32[]{:S(2)}, u32[]{:S(2)}) collective-permute-start(bf16[144,512]{1,0:T(8,128)(2,1)S(1)} %shard_map.61), channel_id=1, source_target_pairs={{0,12},{1,13},{2,14},{3,15},{4,8},{5,9},{6,10},{7,11},{8,4},{9,5},... | collective-permute-start | bytes 442376 | tf_op jit(solution)/shard_map/ppermute | solution.py:118
  36.7 13.1 %collective-permute-start.10 = (bf16[144,512]{1,0:T(8,128)(2,1)S(1)}, bf16[144,512]{1,0:T(8,128)(2,1)S(1)}, u32[]{:S(2)}, u32[]{:S(2)}) collective-permute-start(bf16[144,512]{1,0:T(8,128)(2,1)S(1)} %shard_map.60), channel_id=1, source_target_pairs={{0,8},{1,9},{2,10},{3,11},{4,12},{5,13},{6,14},{7,15},{8,0},{9,1},... | collective-permute-start | bytes 442376 | tf_op jit(solution)/shard_map/ppermute | solution.py:118

commit v2 on v1

--- a/solution.py
+++ b/solution.py
@@ -12,28 +12,70 @@
 log2_e = 1.4426950408889634
 inner = 4
 extra_rows = 16
+tail_rows = 8
 code_span = 240.0
 code_low = -120.0
 
 
-def block_update(state, query, keys, values, limit, scale):
-    shard_keys, width = keys.shape
-    scores = lax.dot_general(keys, query, (((1,), (1,)), ((), ())), preferred_element_type=jnp.float32)
-    key_position = lax.broadcasted_iota(jnp.int32, scores.shape, 0)
-    scores = jnp.where(key_position <= limit, scores, masked_floor)
-    shard_max = jnp.max(scores, axis=0, keepdims=True)
-    weights = jnp.exp2((scores - shard_max) * scale).astype(jnp.bfloat16)
-    ones = jnp.ones((extra_rows, shard_keys), jnp.bfloat16)
-    values_t = jnp.concatenate([values.T, ones], axis=0)
-    sums = lax.dot_general(values_t, weights, (((1,), (0,)), ((), ())), preferred_element_type=jnp.float32)
-    num, den = sums[:width], sums[width : width + 1]
-    if state is None:
-        return shard_max, den, num
-    top, run_den, run_num = state
-    new_top = jnp.maximum(top, shard_max)
-    keep = jnp.exp2((top - new_top) * scale)
-    fresh = jnp.exp2((shard_max - new_top) * scale)
-    return new_top, run_den * keep + den * fresh, run_num * keep + num * fresh
+def attend_tiles(scale, query, keys, values, limits, states, scores_ref, weights_ref, values_ref):
+    rows, width = query.shape
+    shard_keys = keys[0].shape[0]
+    tile = scores_ref.shape[2]
+    chunk = min(512, shard_keys)
+    chunks = shard_keys // chunk
+    scaled = query.astype(jnp.float32) * scale
+    high = scaled.astype(jnp.bfloat16)
+    low = (scaled - high.astype(jnp.float32)).astype(jnp.bfloat16)
+    query_pair = jnp.concatenate([high, low], axis=1)
+    for b, value in enumerate(values):
+        values_ref[b, :width, :] = value[...].T
+        values_ref[b, width:, :] = jnp.ones((extra_rows, shard_keys), jnp.bfloat16)
+    sublane = lax.broadcasted_iota(jnp.int32, (8, tile), 0)
+    tiles = [(b, h) for b in range(len(keys)) for h in range(rows // tile)]
+    count = len(tiles)
+    running, tops = [None] * count, [None] * count
+    states = list(states)
+    for step in range(count + 2):
+        for c in range(chunks):
+            span = slice(c * chunk, (c + 1) * chunk)
+            if step < count:
+                b, h = tiles[step]
+                lanes = slice(h * tile, (h + 1) * tile)
+                key = keys[b][span, :]
+                scores = lax.dot_general(
+                    jnp.concatenate([key, key], axis=1),
+                    query_pair[lanes],
+                    (((1,), (1,)), ((), ())),
+                    preferred_element_type=jnp.float32,
+                ).reshape(chunk // 8, 8, tile)
+                position = lax.broadcasted_iota(jnp.int32, scores.shape, 0) * 8 + c * chunk
+                scores = jnp.where(position <= (limits[b][:, lanes] - sublane)[None], scores, masked_floor)
+                peak = jnp.max(scores, axis=0)
+                running[step] = peak if c == 0 else jnp.maximum(running[step], peak)
+                scores_ref[step % 2, span, :] = scores.reshape(chunk, tile)
+            if 1 <= step <= count:
+                t = step - 1
+                if c == 0:
+                    tops[t] = jnp.max(running[t], axis=0, keepdims=True)
+                weights_ref[t % 2, span, :] = jnp.exp2(scores_ref[t % 2, span, :] - tops[t]).astype(jnp.bfloat16)
+            if step >= 2 and c == min(1, chunks - 1):
+                b, h = tiles[step - 2]
+                shard_max = tops[step - 2]
+                sums = lax.dot_general(
+                    values_ref[b],
+                    weights_ref[step % 2],
+                    (((1,), (0,)), ((), ())),
+                    preferred_element_type=jnp.float32,
+                )
+                num, den = sums[:width], sums[width : width + 1]
+                if states[h] is None:
+                    states[h] = (shard_max, den, num)
+                else:
+                    top, run_den, run_num = states[h]
+                    new_top = jnp.maximum(top, shard_max)
+                    keep, fresh = jnp.exp2(top - new_top), jnp.exp2(shard_max - new_top)
+                    states[h] = (new_top, run_den * keep + den * fresh, run_num * keep + num * fresh)
+    return states
 
 
 def encode(values, level):
@@ -45,7 +87,7 @@
     high = level.astype(jnp.bfloat16).astype(jnp.float32)
     rest = level - high
     middle = rest.astype(jnp.bfloat16).astype(jnp.float32)
-    row = lax.broadcasted_iota(jnp.int32, (extra_rows, lanes), 0)
+    row = lax.broadcasted_iota(jnp.int32, (tail_rows, lanes), 0)
     tail = jnp.where(row == 0, high, jnp.where(row == 1, middle, jnp.where(row == 2, rest - middle, peak)))
     return code.astype(jnp.bfloat16), tail.astype(jnp.bfloat16)
 
@@ -58,35 +100,39 @@
 
 
 def attend_kernel(scale, rows_of, has_state, form, own_rows, *refs):
+    refs, scratch = refs[:-3], refs[-3:]
     limits_ref, q_ref = refs[:2]
-    pair_refs = refs[2 : 2 + 2 * len(rows_of)]
-    rest = refs[2 + 2 * len(rows_of) :]
-    query = q_ref[...]
-    state = None
+    keys = list(refs[2 : 2 + 2 * len(rows_of) : 2])
+    values = list(refs[3 : 3 + 2 * len(rows_of) : 2])
+    rest = list(refs[2 + 2 * len(rows_of) :])
+    rows, width = q_ref.shape
+    tile = scratch[0].shape[2]
+    spans = [slice(at, at + tile) for at in range(0, rows, tile)]
+    states = [None] * len(spans)
     if has_state:
-        state = tuple(ref[...] for ref in rest[:3])
+        states = [tuple(ref[:, span] for ref in rest[:3]) for span in spans]
         rest = rest[3:]
-    for at, row in enumerate(rows_of):
-        keys, values = pair_refs[2 * at][...], pair_refs[2 * at + 1][...]
-        state = block_update(state, query, keys, values, limits_ref[row : row + 1, :], scale)
-    if form == "state":
-        for ref, value in zip(rest, state):
-            ref[...] = value
-        return
-    top, den, num = state
-    width = num.shape[0]
-    level = top * scale + jnp.log2(den)
-    out = num * (1.0 / den)
-    rest = list(rest)
-    if own_rows:
-        out_ref, level_ref = rest[:2]
-        rest = rest[2:]
-        out_ref[...] = out[:, :own_rows]
-        level_ref[...] = level[:, :own_rows]
-    if rest:
-        code, tail = encode(out, level)
-        rest[0][:width, :] = code
-        rest[0][width:, :] = tail
+    limits = [limits_ref[row : row + 1, :] for row in rows_of]
+    states = attend_tiles(scale, q_ref[...], keys, values, limits, states, *scratch)
+    for span, state in zip(spans, states):
+        if form == "state":
+            for ref, value in zip(rest, state):
+                ref[:, span] = value
+            continue
+        top, den, num = state
+        level = top + jnp.log2(den)
+        out = num * (1.0 / den)
+        outs = rest
+        if own_rows:
+            own_span = slice(span.start, min(span.stop, own_rows))
+            if own_span.start < own_span.stop:
+                outs[0][:, own_span] = out[:, : own_span.stop - own_span.start]
+                outs[1][:, own_span] = level[:, : own_span.stop - own_span.start]
+            outs = outs[2:]
+        if outs:
+            code, tail = encode(out, level)
+            outs[0][:width, span] = code
+            outs[0][width:, span] = tail
 
 
 def merge_kernel(count, *refs):
@@ -133,6 +179,7 @@
                 got[k] = swap(got[k ^ low], inner * low)
 
     stage_rows = rows * per_stage
+    tile = 256 if stage_rows % 256 == 0 else stage_rows
 
     limits = (span_offset[0] + positions).reshape(outer, inner, own_tokens)
     limits = lax.dynamic_index_in_dim(limits, place, 1, keepdims=False)
@@ -145,11 +192,11 @@
         return items[0] if len(items) == 1 else jnp.concatenate(items, axis=axis)
 
     vmem = pl.BlockSpec(memory_space=pltpu.VMEM)
-    params = pltpu.CompilerParams(vmem_limit_bytes=40 << 20)
+    params = pltpu.CompilerParams(vmem_limit_bytes=20 << 20)
     pairs = [[cache_keys, cache_values], near_pair]
     stat = jax.ShapeDtypeStruct((1, stage_rows), jnp.float32)
     state_shapes = [stat, stat, jax.ShapeDtypeStruct((head_width, stage_rows), jnp.float32)]
-    packed_shape = jax.ShapeDtypeStruct((head_width + extra_rows, stage_rows), jnp.bfloat16)
+    packed_shape = jax.ShapeDtypeStruct((head_width + tail_rows, stage_rows), jnp.bfloat16)
     own_shapes = [jax.ShapeDtypeStruct((head_width, rows), jnp.float32), jax.ShapeDtypeStruct((1, rows), jnp.float32)]
     chain = [limits]
     states = [None] * len(stages)
@@ -168,6 +215,11 @@
             in_specs=[vmem] * len(operands),
             out_specs=[vmem] * len(shapes),
             out_shape=shapes,
+            scratch_shapes=[
+                pltpu.VMEM((2, shard_keys, tile), jnp.float32),
+                pltpu.VMEM((2, shard_keys, tile), jnp.bfloat16),
+                pltpu.VMEM((len(blocks), head_width + extra_rows, shard_keys), jnp.bfloat16),
+            ],
             compiler_params=params,
         )(*operands)
         chain[0], results = lax.optimization_barrier((chain[0], results))
@@ -187,8 +239,7 @@
     for index in range(len(stages) - 1):
         gather(index)
         ready(index)
-    attend(0, [0], "state")
-    attend(0, [1], "state")
+    attend(0, [0, 1], "state")
     for index in range(1, last):
         if index == last - 1:
             source = stages[index][0]

time: 51 us -> 47 us (0.922)
  Pallas kernels: 17.8 us -> 13.4 us
    pallas_call x9 -> x8, Pallas kernels: 16.7 us -> 12.4 us  [attend(): pl.pallas_call(functools.partial(attend_kernel, scale, [index * inner + b...]
  transfers between devices with their start and end apart: 12 -> 12, of which waited for: 5 -> 5; matrix products, arithmetic and copies ran while one was open for 2% -> 2% of each run, Pallas kernels for 20% -> 16%
where the time goes in v2:
time: 47 us; the launch traced here: 46.9 us
  waiting for transfers between devices  18.4 us (39%)
  Pallas kernels  13.4 us (29%)
  starting transfers between devices  12.1 us (26%)
  local copies, waits for them, and re-layouts  1.33 us (3%)
  between operations  0.84 us (2%)
  other arithmetic  0.77 us (2%)
    ppermute x12, waiting for transfers between devices, swap(): return lax.ppermute(array, 'ctx', [(i, i ^ step) for i in range(size)])  18.4 us
    pallas_call x8, Pallas kernels, attend(): pl.pallas_call(functools.partial(attend_kernel, scale, [index * inner + b...  12.4 us
    ppermute x12, starting transfers between devices, swap(): return lax.ppermute(array, 'ctx', [(i, i ^ step) for i in range(size)])  12.1 us
    pallas_call x1, Pallas kernels, local(): pl.pallas_call(functools.partial(merge_kernel, outer), in_specs=[vmem] *...  1.03 us
    unnamed x6, local copies, waits for them, and re-layouts  0.95 us
  transfers between devices with their start and end apart: 12, of which 5 were waited for; matrix products, arithmetic and copies ran while one was open for 2% of the time, Pallas kernels for 16%

profile of v2, /device:TPU:0, one launch (start us, length us, event | category | flops | bytes accessed | tf_op | source)
XLA Modules:
  0.0 46.9 jit_solution(10077558069480642366)
XLA Ops:
  0.0 0.0 copy-start
  0.0 0.5 %collective-permute-start = (bf16[1024,128]{1,0:T(8,128)(2,1)}, bf16[1024,128]{1,0:T(8,128)(2,1)S(1)}, u32[]{:S(2)}, u32[]{:S(2)}) collective-permute-start(bf16[1024,128]{1,0:T(8,128)(2,1)} %refs_2_.7), channel_id=1, source_target_pairs={{0,1},{1,0},{2,3},{3,2},{4,5},{5,4},{6,7},{7,6},{8,9},{9,8},{10,11... | collective-permute-start | bytes 786440 | tf_op jit(solution)/shard_map/ppermute | solution.py:164
  0.5 2.6 %collective-permute-start.4 = (bf16[1024,128]{1,0:T(8,128)(2,1)}, bf16[1024,128]{1,0:T(8,128)(2,1)S(1)}, u32[]{:S(2)}, u32[]{:S(2)}) collective-permute-start(bf16[1024,128]{1,0:T(8,128)(2,1)} %refs_2_.7), channel_id=1, source_target_pairs={{0,2},{1,3},{2,0},{3,1},{4,6},{5,7},{6,4},{7,5},{8,10},{9,11},{10,... | collective-permute-start | bytes 786440 | tf_op jit(solution)/shard_map/ppermute | solution.py:164
  3.1 0.2 collective-permute-start.1
  3.2 0.3 collective-permute-start.5
  3.5 2.8 %collective-permute-start.3 = (bf16[512,128]{1,0:T(8,128)(2,1)}, bf16[512,128]{1,0:T(8,128)(2,1)S(1)}, u32[]{:S(2)}, u32[]{:S(2)}) collective-permute-start(bf16[512,128]{1,0:T(8,128)(2,1)} %bitcast.12), channel_id=1, source_target_pairs={{0,8},{1,9},{2,10},{3,11},{4,12},{5,13},{6,14},{7,15},{8,0},{9,1},... | collective-permute-start | bytes 393224 | tf_op jit(solution)/shard_map/ppermute | solution.py:164
  7.0 0.7 %broadcast_add_fusion = s32[512]{0:T(512)S(1)} fusion(s32[512]{0:T(512)} %param.9, s32[]{:T(128)} %bitcast.11), kind=kLoop, calls=%fused_computation.6 | loop fusion | flops 512 | bytes 4100 | tf_op jit(solution)/shard_map/add | solution.py:184
  7.7 0.1 reshape.22
  7.8 0.1 sub.31
  7.9 0.1 broadcast_in_dim.4
  8.0 0.0 copy-start.2
  8.0 0.1 sub.27
  8.1 0.0 collective-permute-done.refs_4_
  8.1 1.6 %collective-permute-start.2 = (bf16[512,128]{1,0:T(8,128)(2,1)}, bf16[512,128]{1,0:T(8,128)(2,1)S(1)}, u32[]{:S(2)}, u32[]{:S(2)}) collective-permute-start(bf16[512,128]{1,0:T(8,128)(2,1)} %bitcast.13), channel_id=1, source_target_pairs={{0,4},{1,5},{2,6},{3,7},{4,0},{5,1},{6,2},{7,3},{8,12},{9,13},{10,... | collective-permute-start | bytes 393224 | tf_op jit(solution)/shard_map/ppermute | solution.py:164
  9.8 0.1 broadcast_subtract_fusion.refs_0_
  9.8 0.0 collective-permute-done.1.refs_5_
  9.8 0.0 copy-done
  9.8 0.0 copy-done.2
  9.8 0.0 copy-start.1
  9.9 0.9 %copy-done.1 = bf16[1024,128]{1,0:T(8,128)(2,1)S(1)} copy-done((bf16[1024,128]{1,0:T(8,128)(2,1)S(1)}, bf16[1024,128]{1,0:T(8,128)(2,1)}, u32[]{:S(2)}) %copy-start.1) | copy-done | bytes 262168
  10.8 1.5 %shard_map.55 = (f32[1,512]{1,0:T(1,128)S(1)}, f32[1,512]{1,0:T(1,128)S(1)}, f32[128,512]{1,0:T(8,128)S(1)}) custom-call(s32[16,512]{1,0:T(8,128)S(1)} %broadcast_subtract_fusion.refs_0_, bf16[512,128]{1,0:T(8,128)(2,1)S(1)} %bitcast.14, bf16[1024,128]{1,0:T(8,128)(2,1)S(1)} %copy-done, bf16[1024,128]{1,0:T(8,128)(2,1)S(1)} %copy-done.1, ...), custom_call_target="tpu_custom_call" | custom-call | tf_op jit(solution)/shard_map/pallas_call | solution.py:211
  12.3 2.8 %collective-permute-done.2.refs_1_ = bf16[512,128]{1,0:T(8,128)(2,1)S(1)} collective-permute-done((bf16[512,128]{1,0:T(8,128)(2,1)}, bf16[512,128]{1,0:T(8,128)(2,1)S(1)}, u32[]{:S(2)}, u32[]{:S(2)}) %collective-permute-start.2) | collective-permute-done | bytes 131104 | tf_op jit(solution)/shard_map/ppermute | solution.py:164
  15.1 1.5 %shard_map.56 = (f32[1,512]{1,0:T(1,128)S(1)}, f32[1,512]{1,0:T(1,128)S(1)}, f32[128,512]{1,0:T(8,128)S(1)}) custom-call(s32[16,512]{1,0:T(8,128)S(1)} %broadcast_subtract_fusion.refs_0_, bf16[512,128]{1,0:T(8,128)(2,1)S(1)} %collective-permute-done.2.refs_1_, bf16[1024,128]{1,0:T(8,128)(2,1)S(1)} %copy-done, bf16[1024,128]{1,0:T(8,128)(2,1)S(1)} %copy-done.1, ...), custom_call_target="tpu_custom_call" | custom-call | tf_op jit(solution)/shard_map/pallas_call | solution.py:211
  16.6 0.0 collective-permute-done.3.refs_1_
  16.7 1.5 %shard_map.57 = (f32[1,512]{1,0:T(1,128)S(1)}, f32[1,512]{1,0:T(1,128)S(1)}, f32[128,512]{1,0:T(8,128)S(1)}) custom-call(s32[16,512]{1,0:T(8,128)S(1)} %broadcast_subtract_fusion.refs_0_, bf16[512,128]{1,0:T(8,128)(2,1)S(1)} %collective-permute-done.3.refs_1_, bf16[1024,128]{1,0:T(8,128)(2,1)S(1)} %copy-done, bf16[1024,128]{1,0:T(8,128)(2,1)S(1)} %copy-done.1, ...), custom_call_target="tpu_custom_call" | custom-call | tf_op jit(solution)/shard_map/pallas_call | solution.py:211
  18.2 0.0 collective-permute-done.4.refs_2_
  18.2 0.0 collective-permute-done.5.refs_3_
  18.2 0.1 collective-permute-start.7
  18.3 0.5 %collective-permute-start.8 = (bf16[1024,128]{1,0:T(8,128)(2,1)S(1)}, bf16[1024,128]{1,0:T(8,128)(2,1)S(1)}, u32[]{:S(2)}, u32[]{:S(2)}) collective-permute-start(bf16[1024,128]{1,0:T(8,128)(2,1)S(1)} %collective-permute-done.5.refs_3_), channel_id=1, source_target_pairs={{0,1},{1,0},{2,3},{3,2},{4,5},{5,4},{6,7},{7,6},{8,9},{9,8},{10,11... | collective-permute-start | bytes 786440 | tf_op jit(solution)/shard_map/ppermute | solution.py:164
  18.8 0.0 collective-permute-start.6
  18.8 5.5 %collective-permute-done.6.refs_1_ = bf16[512,128]{1,0:T(8,128)(2,1)S(1)} collective-permute-done((bf16[512,128]{1,0:T(8,128)(2,1)S(1)}, bf16[512,128]{1,0:T(8,128)(2,1)S(1)}, u32[]{:S(2)}, u32[]{:S(2)}) %collective-permute-start.6) | collective-permute-done | bytes 131104 | tf_op jit(solution)/shard_map/ppermute | solution.py:164
  24.3 1.5 %shard_map.58 = (f32[1,512]{1,0:T(1,128)S(1)}, f32[1,512]{1,0:T(1,128)S(1)}, f32[128,512]{1,0:T(8,128)S(1)}) custom-call(s32[16,512]{1,0:T(8,128)S(1)} %broadcast_subtract_fusion.refs_0_, bf16[512,128]{1,0:T(8,128)(2,1)S(1)} %collective-permute-done.6.refs_1_, bf16[1024,128]{1,0:T(8,128)(2,1)S(1)} %copy-done, bf16[1024,128]{1,0:T(8,128)(2,1)S(1)} %copy-done.1, ...), custom_call_target="tpu_custom_call" | custom-call | tf_op jit(solution)/shard_map/pallas_call | solution.py:211
  25.8 0.0 collective-permute-done.7.refs_4_
  25.8 0.0 collective-permute-done.8.refs_5_
  25.8 1.6 %shard_map.59 = bf16[136,512]{1,0:T(8,128)(2,1)S(1)} custom-call(s32[16,512]{1,0:T(8,128)S(1)} %broadcast_subtract_fusion.refs_0_, bf16[512,128]{1,0:T(8,128)(2,1)S(1)} %collective-permute-done.3.refs_1_, bf16[1024,128]{1,0:T(8,128)(2,1)S(1)} %collective-permute-done.4.refs_2_, bf16[1024,128]{1,0:T(8,128)(2,1)S(1)} %collective-permute-done.5.refs_3_, ...), custom_call_target="tpu_custom_call" | custom-call | tf_op jit(solution)/shard_map/pallas_call | solution.py:211
  27.4 1.6 %shard_map.60 = bf16[136,512]{1,0:T(8,128)(2,1)S(1)} custom-call(s32[16,512]{1,0:T(8,128)S(1)} %broadcast_subtract_fusion.refs_0_, bf16[512,128]{1,0:T(8,128)(2,1)S(1)} %collective-permute-done.6.refs_1_, bf16[1024,128]{1,0:T(8,128)(2,1)S(1)} %collective-permute-done.4.refs_2_, bf16[1024,128]{1,0:T(8,128)(2,1)S(1)} %collective-permute-done.5.refs_3_, ...), custom_call_target="tpu_custom_call" | custom-call | tf_op jit(solution)/shard_map/pallas_call | solution.py:211
  29.0 1.6 %shard_map.61 = bf16[136,512]{1,0:T(8,128)(2,1)S(1)} custom-call(s32[16,512]{1,0:T(8,128)S(1)} %broadcast_subtract_fusion.refs_0_, bf16[512,128]{1,0:T(8,128)(2,1)S(1)} %collective-permute-done.2.refs_1_, bf16[1024,128]{1,0:T(8,128)(2,1)S(1)} %collective-permute-done.4.refs_2_, bf16[1024,128]{1,0:T(8,128)(2,1)S(1)} %collective-permute-done.5.refs_3_, ...), custom_call_target="tpu_custom_call" | custom-call | tf_op jit(solution)/shard_map/pallas_call | solution.py:211
  30.6 0.3 collective-permute-start.9
  31.0 2.5 %collective-permute-start.11 = (bf16[136,512]{1,0:T(8,128)(2,1)S(1)}, bf16[136,512]{1,0:T(8,128)(2,1)S(1)}, u32[]{:S(2)}, u32[]{:S(2)}) collective-permute-start(bf16[136,512]{1,0:T(8,128)(2,1)S(1)} %shard_map.60), channel_id=1, source_target_pairs={{0,12},{1,13},{2,14},{3,15},{4,8},{5,9},{6,10},{7,11},{8,4},{9,5},... | collective-permute-start | bytes 417800 | tf_op jit(solution)/shard_map/ppermute | solution.py:164
  33.5 0.7 %collective-permute-start.10 = (bf16[136,512]{1,0:T(8,128)(2,1)S(1)}, bf16[136,512]{1,0:T(8,128)(2,1)S(1)}, u32[]{:S(2)}, u32[]{:S(2)}) collective-permute-start(bf16[136,512]{1,0:T(8,128)(2,1)S(1)} %shard_map.59), channel_id=1, source_target_pairs={{0,8},{1,9},{2,10},{3,11},{4,12},{5,13},{6,14},{7,15},{8,0},{9,1},... | collective-permute-start | bytes 417800 | tf_op jit(solution)/shard_map/ppermute | solution.py:164
  34.2 1.5 %shard_map.62 = (f32[128,512]{1,0:T(8,128)S(1)}, f32[1,512]{1,0:T(1,128)S(1)}) custom-call(s32[16,512]{1,0:T(8,128)S(1)} %broadcast_subtract_fusion.refs_0_, bf16[512,128]{1,0:T(8,128)(2,1)S(1)} %bitcast.15, bf16[1024,128]{1,0:T(8,128)(2,1)S(1)} %collective-permute-done.4.refs_2_, bf16[1024,128]{1,0:T(8,128)(2,1)S(1)} %collective-permute-done.5.refs_3_, ...), custom_call_target="tpu_custom_call" | custom-call | tf_op jit(solution)/shard_map/pallas_call | solution.py:211
  35.7 1.3 %collective-permute-done.9.refs_2_ = bf16[136,512]{1,0:T(8,128)(2,1)S(1)} collective-permute-done((bf16[136,512]{1,0:T(8,128)(2,1)S(1)}, bf16[136,512]{1,0:T(8,128)(2,1)S(1)}, u32[]{:S(2)}, u32[]{:S(2)}) %collective-permute-start.9) | collective-permute-done | bytes 139296 | tf_op jit(solution)/shard_map/ppermute | solution.py:164
  37.0 4.1 %collective-permute-done.11.refs_4_ = bf16[136,512]{1,0:T(8,128)(2,1)S(1)} collective-permute-done((bf16[136,512]{1,0:T(8,128)(2,1)S(1)}, bf16[136,512]{1,0:T(8,128)(2,1)S(1)}, u32[]{:S(2)}, u32[]{:S(2)}) %collective-permute-start.11) | collective-permute-done | bytes 139296 | tf_op jit(solution)/shard_map/ppermute | solution.py:164
  41.1 4.8 %collective-permute-done.10.refs_3_ = bf16[136,512]{1,0:T(8,128)(2,1)S(1)} collective-permute-done((bf16[136,512]{1,0:T(8,128)(2,1)S(1)}, bf16[136,512]{1,0:T(8,128)(2,1)S(1)}, u32[]{:S(2)}, u32[]{:S(2)}) %collective-permute-start.10) | collective-permute-done | bytes 139296 | tf_op jit(solution)/shard_map/ppermute | solution.py:164
  45.8 1.0 %merge.1 = bf16[512,128]{1,0:T(8,128)(2,1)} custom-call(f32[128,512]{1,0:T(8,128)S(1)} %get-tuple-element.86.refs_0_, f32[1,512]{1,0:T(1,128)S(1)} %get-tuple-element.87.refs_1_, bf16[136,512]{1,0:T(8,128)(2,1)S(1)} %collective-permute-done.9.refs_2_, bf16[136,512]{1,0:T(8,128)(2,1)S(1)} %collective-permute-done.10.refs_3_, ...), custom_call_target="tpu_custom_call" | custom-call | tf_op jit(solution)/shard_map/merge/pallas_call | solution.py:266
  (6 shorter events, 0.1 us)
Async XLA Ops:
  0.0 9.8 %copy-start = (bf16[1024,128]{1,0:T(8,128)(2,1)S(1)}, bf16[1024,128]{1,0:T(8,128)(2,1)}, u32[]{:S(2)}) copy-start(bf16[1024,128]{1,0:T(8,128)(2,1)} %refs_2_.7) | copy-start | bytes 786436
  0.0 8.1 %collective-permute-start = (bf16[1024,128]{1,0:T(8,128)(2,1)}, bf16[1024,128]{1,0:T(8,128)(2,1)S(1)}, u32[]{:S(2)}, u32[]{:S(2)}) collective-permute-start(bf16[1024,128]{1,0:T(8,128)(2,1)} %refs_2_.7), channel_id=1, source_target_pairs={{0,1},{1,0},{2,3},{3,2},{4,5},{5,4},{6,7},{7,6},{8,9},{9,8},{10,11... | collective-permute-start | bytes 786440 | tf_op jit(solution)/shard_map/ppermute | solution.py:164
  0.5 17.7 %collective-permute-start.4 = (bf16[1024,128]{1,0:T(8,128)(2,1)}, bf16[1024,128]{1,0:T(8,128)(2,1)S(1)}, u32[]{:S(2)}, u32[]{:S(2)}) collective-permute-start(bf16[1024,128]{1,0:T(8,128)(2,1)} %refs_2_.7), channel_id=1, source_target_pairs={{0,2},{1,3},{2,0},{3,1},{4,6},{5,7},{6,4},{7,5},{8,10},{9,11},{10,... | collective-permute-start | bytes 786440 | tf_op jit(solution)/shard_map/ppermute | solution.py:164
  3.1 6.8 %collective-permute-start.1 = (bf16[1024,128]{1,0:T(8,128)(2,1)}, bf16[1024,128]{1,0:T(8,128)(2,1)S(1)}, u32[]{:S(2)}, u32[]{:S(2)}) collective-permute-start(bf16[1024,128]{1,0:T(8,128)(2,1)} %refs_3_.7), channel_id=1, source_target_pairs={{0,1},{1,0},{2,3},{3,2},{4,5},{5,4},{6,7},{7,6},{8,9},{9,8},{10,11... | collective-permute-start | bytes 786440 | tf_op jit(solution)/shard_map/ppermute | solution.py:164
  3.2 15.0 %collective-permute-start.5 = (bf16[1024,128]{1,0:T(8,128)(2,1)}, bf16[1024,128]{1,0:T(8,128)(2,1)S(1)}, u32[]{:S(2)}, u32[]{:S(2)}) collective-permute-start(bf16[1024,128]{1,0:T(8,128)(2,1)} %refs_3_.7), channel_id=1, source_target_pairs={{0,2},{1,3},{2,0},{3,1},{4,6},{5,7},{6,4},{7,5},{8,10},{9,11},{10,... | collective-permute-start | bytes 786440 | tf_op jit(solution)/shard_map/ppermute | solution.py:164
  3.5 13.1 %collective-permute-start.3 = (bf16[512,128]{1,0:T(8,128)(2,1)}, bf16[512,128]{1,0:T(8,128)(2,1)S(1)}, u32[]{:S(2)}, u32[]{:S(2)}) collective-permute-start(bf16[512,128]{1,0:T(8,128)(2,1)} %bitcast.12), channel_id=1, source_target_pairs={{0,8},{1,9},{2,10},{3,11},{4,12},{5,13},{6,14},{7,15},{8,0},{9,1},... | collective-permute-start | bytes 393224 | tf_op jit(solution)/shard_map/ppermute | solution.py:164
  8.0 1.9 %copy-start.2 = (bf16[32,16,128]{2,1,0:T(8,128)(2,1)S(1)}, bf16[32,16,128]{2,1,0:T(8,128)(2,1)}, u32[]{:S(2)}) copy-start(bf16[32,16,128]{2,1,0:T(8,128)(2,1)} %param.5) | copy-start | bytes 393220
  8.1 7.0 %collective-permute-start.2 = (bf16[512,128]{1,0:T(8,128)(2,1)}, bf16[512,128]{1,0:T(8,128)(2,1)S(1)}, u32[]{:S(2)}, u32[]{:S(2)}) collective-permute-start(bf16[512,128]{1,0:T(8,128)(2,1)} %bitcast.13), channel_id=1, source_target_pairs={{0,4},{1,5},{2,6},{3,7},{4,0},{5,1},{6,2},{7,3},{8,12},{9,13},{10,... | collective-permute-start | bytes 393224 | tf_op jit(solution)/shard_map/ppermute | solution.py:164
  9.8 1.0 %copy-start.1 = (bf16[1024,128]{1,0:T(8,128)(2,1)S(1)}, bf16[1024,128]{1,0:T(8,128)(2,1)}, u32[]{:S(2)}) copy-start(bf16[1024,128]{1,0:T(8,128)(2,1)} %refs_3_.7) | copy-start | bytes 786436
  18.2 7.6 %collective-permute-start.7 = (bf16[1024,128]{1,0:T(8,128)(2,1)S(1)}, bf16[1024,128]{1,0:T(8,128)(2,1)S(1)}, u32[]{:S(2)}, u32[]{:S(2)}) collective-permute-start(bf16[1024,128]{1,0:T(8,128)(2,1)S(1)} %collective-permute-done.4.refs_2_), channel_id=1, source_target_pairs={{0,1},{1,0},{2,3},{3,2},{4,5},{5,4},{6,7},{7,6},{8,9},{9,8},{10,11... | collective-permute-start | bytes 786440 | tf_op jit(solution)/shard_map/ppermute | solution.py:164
  18.3 7.5 %collective-permute-start.8 = (bf16[1024,128]{1,0:T(8,128)(2,1)S(1)}, bf16[1024,128]{1,0:T(8,128)(2,1)S(1)}, u32[]{:S(2)}, u32[]{:S(2)}) collective-permute-start(bf16[1024,128]{1,0:T(8,128)(2,1)S(1)} %collective-permute-done.5.refs_3_), channel_id=1, source_target_pairs={{0,1},{1,0},{2,3},{3,2},{4,5},{5,4},{6,7},{7,6},{8,9},{9,8},{10,11... | collective-permute-start | bytes 786440 | tf_op jit(solution)/shard_map/ppermute | solution.py:164
  18.8 5.5 %collective-permute-start.6 = (bf16[512,128]{1,0:T(8,128)(2,1)S(1)}, bf16[512,128]{1,0:T(8,128)(2,1)S(1)}, u32[]{:S(2)}, u32[]{:S(2)}) collective-permute-start(bf16[512,128]{1,0:T(8,128)(2,1)S(1)} %collective-permute-done.3.refs_1_), channel_id=1, source_target_pairs={{0,4},{1,5},{2,6},{3,7},{4,0},{5,1},{6,2},{7,3},{8,12},{9,13},{10,... | collective-permute-start | bytes 393224 | tf_op jit(solution)/shard_map/ppermute | solution.py:164
  30.6 6.3 %collective-permute-start.9 = (bf16[136,512]{1,0:T(8,128)(2,1)S(1)}, bf16[136,512]{1,0:T(8,128)(2,1)S(1)}, u32[]{:S(2)}, u32[]{:S(2)}) collective-permute-start(bf16[136,512]{1,0:T(8,128)(2,1)S(1)} %shard_map.61), channel_id=1, source_target_pairs={{0,4},{1,5},{2,6},{3,7},{4,0},{5,1},{6,2},{7,3},{8,12},{9,13},{10,... | collective-permute-start | bytes 417800 | tf_op jit(solution)/shard_map/ppermute | solution.py:164
  31.0 10.1 %collective-permute-start.11 = (bf16[136,512]{1,0:T(8,128)(2,1)S(1)}, bf16[136,512]{1,0:T(8,128)(2,1)S(1)}, u32[]{:S(2)}, u32[]{:S(2)}) collective-permute-start(bf16[136,512]{1,0:T(8,128)(2,1)S(1)} %shard_map.60), channel_id=1, source_target_pairs={{0,12},{1,13},{2,14},{3,15},{4,8},{5,9},{6,10},{7,11},{8,4},{9,5},... | collective-permute-start | bytes 417800 | tf_op jit(solution)/shard_map/ppermute | solution.py:164
  33.5 12.4 %collective-permute-start.10 = (bf16[136,512]{1,0:T(8,128)(2,1)S(1)}, bf16[136,512]{1,0:T(8,128)(2,1)S(1)}, u32[]{:S(2)}, u32[]{:S(2)}) collective-permute-start(bf16[136,512]{1,0:T(8,128)(2,1)S(1)} %shard_map.59), channel_id=1, source_target_pairs={{0,8},{1,9},{2,10},{3,11},{4,12},{5,13},{6,14},{7,15},{8,0},{9,1},... | collective-permute-start | bytes 417800 | tf_op jit(solution)/shard_map/ppermute | solution.py:164
